TPU v7x, 256 devices: a whole 4x4x8 slice. The times are simulated.
256 devices in a mesh: dp: 2 (over core), tm: 32 (over z, y), space: 4 (over x).
Axes of the slice: x: 4, y: 4, z: 8, core: 2. Of those that a mesh axis runs over, the one named last changes fastest.
Arguments:
- latents: bfloat16 [2, 64, 8, 80, 512], P('dp', 'tm', 'space'), may hold values from -6 to 6
- norm_gain: float32 [512], replicated, may hold values from 0.25 to 1.75
- kernel: bfloat16 [13824, 512], P(None, 'dp'), may hold values from -0.0546875 to 0.0546875
- conv_bias: float32 [512], replicated, may hold values from -3 to 3
- out_grad: bfloat16 [2, 64, 8, 80, 512], P('dp', 'tm', 'space'), may hold values from -6 to 6
Outputs:
- block_out: bfloat16 [2, 64, 8, 80, 512], P('dp', 'tm', 'space')
- latent_grad: bfloat16 [2, 64, 8, 80, 512], P('dp', 'tm', 'space')
- kernel_grad: float32 [13824, 512], P('tm', 'dp')
- gain_grad: float32 [512], replicated
- bias_grad: float32 [512], replicated
All inputs are finite; a program needn't handle non-finite values.
Results may differ from a plain program's by a relative error of at most 0.0029.
Values may be sent and summed in bfloat16 or wider, within the bound.
No kernel may reach another device: no remote copies, remote signals or barrier semaphores. Data moves between devices by JAX's collectives and lax.ppermute only.
A program may use at most 128 MiB of HBM per device.

v0:
```python
import jax
import jax.numpy as jnp
from jax import lax
from jax.sharding import PartitionSpec as P


def shifted(block, axis, distance):
    devices = range(lax.axis_size(axis))
    route = [(i - distance, i) for i in devices if i - distance in devices]
    return lax.ppermute(block, axis, route)


def padded(block, sides, width):
    for axis, dim in sides:
        count = lax.axis_size(axis)
        forward = [(i, i + 1) for i in range(count - 1)]
        backward = [(target, source) for source, target in forward]
        low = lax.ppermute(
            lax.slice_in_dim(block, block.shape[dim] - width, None, axis=dim), axis, forward
        )
        high = lax.ppermute(lax.slice_in_dim(block, 0, width, axis=dim), axis, backward)
        block = jnp.concatenate([low, block, high], axis=dim)
    return block


def tap_columns(extended, frame_count, row_count, col_count, flipped):
    pieces = []
    for tap_t in range(3):
        for tap_h in range(3):
            for tap_w in range(3):
                if flipped:
                    start_t, start_h, start_w = (2 - tap_t, 2 - tap_h, 2 - tap_w)
                else:
                    start_t, start_h, start_w = (tap_t, tap_h, tap_w)
                pieces.append(
                    extended[
                        :,
                        start_t : start_t + frame_count,
                        start_h : start_h + row_count,
                        start_w : start_w + col_count,
                        :,
                    ]
                )
    stacked = jnp.concatenate(pieces, axis=-1)
    return stacked.reshape(-1, stacked.shape[-1])


def pad_columns(extended):
    return jnp.pad(extended, ((0, 0), (0, 0), (0, 0), (1, 1), (0, 0)))


def on_device(latents, norm_gain, kernel, conv_bias, out_grad):
    chans = latents.shape[-1]
    half_cols = kernel.shape[1]
    clip_local, frame_count, row_count, col_count = (
        latents.shape[0],
        latents.shape[1],
        latents.shape[2],
        latents.shape[3],
    )
    cell_total = (
        clip_local
        * frame_count
        * row_count
        * col_count
        * lax.axis_size("dp")
        * lax.axis_size("tm")
        * lax.axis_size("space")
    )
    grad_scale = 1.0 / jnp.sqrt(jnp.float32(cell_total))
    floats = latents.astype(jnp.float32)
    scale = lax.rsqrt(jnp.mean(floats * floats, axis=-1, keepdims=True) + 1e-06)
    normed = floats * scale
    pre_act = normed * norm_gain
    act = jax.nn.silu(pre_act).astype(jnp.bfloat16)
    grad_pair = lax.all_to_all(out_grad, "dp", split_axis=4, concat_axis=0, tiled=True)
    earlier = shifted(act, "tm", 1)
    joined = jnp.concatenate([earlier, act], axis=1)
    act_ext = padded(joined, (("space", 2),), 1)
    later = shifted(grad_pair, "tm", -1)
    joined_grad = jnp.concatenate([grad_pair, later], axis=1)
    grad_ext = padded(joined_grad, (("space", 2),), 1)
    act_pair = lax.all_gather(act_ext, "dp", axis=0, tiled=True)
    pair_clips = act_pair.shape[0]
    act_taps = tap_columns(pad_columns(act_pair), frame_count, row_count, col_count, False)
    conv_part = jnp.dot(act_taps, kernel, preferred_element_type=jnp.float32)
    conv_part = conv_part.reshape(pair_clips, frame_count, row_count, col_count, half_cols)
    conv = lax.all_to_all(conv_part, "dp", split_axis=0, concat_axis=4, tiled=True)
    block_out = (floats + conv + conv_bias).astype(jnp.bfloat16)
    kernel_local = (
        lax.dot_general(
            act_taps,
            grad_pair.reshape(-1, half_cols),
            (((0,), (0,)), ((), ())),
            preferred_element_type=jnp.float32,
        )
        * grad_scale
    )
    flipped_kernel = jnp.transpose(kernel.reshape(-1, chans, half_cols), (0, 2, 1)).reshape(
        -1, chans
    )
    grad_taps = tap_columns(pad_columns(grad_ext), frame_count, row_count, col_count, True)
    partial_grad = jnp.dot(grad_taps, flipped_kernel, preferred_element_type=jnp.float32)
    partial_grad = partial_grad.reshape(pair_clips, frame_count, row_count, col_count, chans)
    act_grad = lax.psum_scatter(partial_grad, "dp", scatter_dimension=0, tiled=True)
    grads = out_grad.astype(jnp.float32)
    bias_local = jnp.sum(grads.reshape(-1, chans), axis=0) * grad_scale
    sig = jax.nn.sigmoid(pre_act)
    pre_grad = act_grad * sig * (1.0 + pre_act * (1.0 - sig))
    gain_local = jnp.sum((pre_grad * normed).reshape(-1, chans), axis=0) * grad_scale
    normed_grad = pre_grad * norm_gain
    latent_grad = grads + scale * (
        normed_grad - normed * jnp.mean(normed_grad * normed, axis=-1, keepdims=True)
    )
    gain_grad, bias_grad = lax.psum((gain_local, bias_local), ("dp", "tm", "space"))
    row_part = lax.psum_scatter(kernel_local, "tm", scatter_dimension=0, tiled=True)
    kernel_grad = lax.psum(row_part, "space")
    return (block_out, latent_grad.astype(jnp.bfloat16), kernel_grad, gain_grad, bias_grad)


def solution(mesh):
    in_specs = (
        P("dp", "tm", "space", None, None),
        P(),
        P(None, "dp"),
        P(),
        P("dp", "tm", "space", None, None),
    )
    out_specs = (
        P("dp", "tm", "space", None, None),
        P("dp", "tm", "space", None, None),
        P("tm", "dp"),
        P(),
        P(),
    )
    return jax.shard_map(
        on_device, mesh=mesh, in_specs=in_specs, out_specs=out_specs, check_vma=False
    )
```

profile of v0, /device:TPU:8, one launch (start us, length us, event | category | flops | bytes accessed | tf_op | source)
XLA Modules:
  0.0 441.9 jit_solution(11372110334327910266)
XLA Ops:
  7.2 1.3 copy.20
  8.5 4.2 all_to_all.36
  13.0 4.1 collective-permute-start.3
  17.1 7.6 %collective-permute-done.3 = bf16[2,2,2,80,256]{4,3,2,1,0:T(8,128)(2,1)S(1)} collective-permute-done((bf16[2,2,2,80,256]{4,3,2,1,0:T(8,128)(2,1)S(1)}, bf16[2,2,2,80,256]{4,3,2,1,0:T(8,128)(2,1)S(1)}, u32[]{:S(2)}, u32[]{:S(2)}) %collective-permute-start.3) | collective-permute-done | bytes 327712 | tf_op jit(solution)/shard_map/ppermute | solution.py:10
  24.7 3.4 collective-permute-start.4
  28.2 1.3 collective-permute-start.5
  29.5 10.3 %copy.23 = bf16[27,256,512]{2,1,0:T(8,128)(2,1)} copy(bf16[27,256,512]{1,2,0:T(8,128)(2,1)} %bitcast.37) | data formatting | bytes 14155776 | tf_op jit(solution)/shard_map/transpose | solution.py:99
  42.0 0.9 slice-done
  42.9 1.1 slice-done.1
  44.0 5.8 %fusion.31 = f32[2,2,2,80,512]{4,3,2,1,0:T(8,128)} fusion(bf16[2,2,2,80,6912]{4,3,2,1,0:T(8,128)(2,1)S(1)} %slice_dynamic-update-slice_fusion.27, bf16[6912,512,1,1,1]{1,0,4,3,2:T(8,128)(2,1)S(1)} %bitcast.40), kind=kOutput, calls=%fused_computation.109 | convolution fusion | flops 4529848320 | bytes 17235968 | tf_op jit(solution)/shard_map/dot_general | solution.py:103
  50.1 20.0 %reduce-scatter.3.cloned.1.call-done = f32[1,2,2,80,512]{4,3,2,1,0:T(8,128)} async-done(((f32[2,2,2,80,512]{4,3,2,1,0:T(8,128)}), f32[1,2,2,80,512]{4,3,2,1,0:T(8,128)}) %reduce-scatter.3.cloned.1.call-update) | async-done | bytes 655376 | tf_op jit(solution)/shard_map/reduce_scatter | solution.py:105
  70.1 1.6 fusion.23
  71.7 2.4 fusion.13
  74.1 3.4 collective-permute-start
  77.5 8.2 %collective-permute-done = bf16[1,2,2,80,512]{4,3,2,1,0:T(8,128)(2,1)S(1)} collective-permute-done((bf16[1,2,2,80,512]{4,3,2,1,0:T(8,128)(2,1)S(1)}, bf16[1,2,2,80,512]{4,3,2,1,0:T(8,128)(2,1)S(1)}, u32[]{:S(2)}, u32[]{:S(2)}) %collective-permute-start) | collective-permute-done | bytes 327712 | tf_op jit(solution)/shard_map/ppermute | solution.py:10
  85.8 3.4 collective-permute-start.1
  89.2 1.3 collective-permute-start.2
  90.5 5.1 %collective-permute-done.1 = bf16[1,4,1,80,512]{4,3,2,1,0:T(8,128)(2,1)S(1)} collective-permute-done((bf16[1,4,1,80,512]{4,3,2,1,0:T(8,128)(2,1)S(1)}, bf16[1,4,1,80,512]{4,3,2,1,0:T(8,128)(2,1)S(1)}, u32[]{:S(2)}, u32[]{:S(2)}) %collective-permute-start.1) | collective-permute-done | bytes 327712 | tf_op jit(solution)/shard_map/ppermute | solution.py:18
  95.6 4.1 collective-permute-done.2
  99.7 1.2 pad_maximum_fusion
  101.2 18.5 %all-gather.2.cloned.1.call-done = bf16[2,4,4,80,512]{4,3,2,1,0:T(8,128)(2,1)} async-done(((bf16[1,4,4,80,512]{4,3,2,1,0:T(8,128)(2,1)}), bf16[2,4,4,80,512]{4,3,2,1,0:T(8,128)(2,1)}) %all-gather.2.cloned.1.call-update) | async-done | bytes 2621456 | tf_op jit(solution)/shard_map/all_gather | solution.py:83
  119.7 1.4 slice_dynamic-update-slice_fusion.26
  121.0 1.1 slice_dynamic-update-slice_fusion.8
  122.2 1.2 slice_dynamic-update-slice_fusion.25
  126.4 6.1 %copy-done.3 = bf16[2,2,2,80,13824]{4,3,2,1,0:T(8,128)(2,1)} copy-done((bf16[2,2,2,80,13824]{4,3,2,1,0:T(8,128)(2,1)}, bf16[2,2,2,80,13824]{4,3,2,1,0:T(8,128)(2,1)S(1)}, u32[]{:S(2)}) %copy-start.3) | copy-done | bytes 17694744
  132.5 9.0 %convolution_multiply_fusion = f32[13824,256]{1,0:T(8,128)} fusion(bf16[640,13824]{1,0:T(8,128)(2,1)S(1)} %bitcast.44, bf16[640,256]{1,0:T(8,128)(2,1)S(1)} %bitcast.36), kind=kOutput, calls=%fused_computation | convolution fusion | flops 4533387264 | bytes 32178176 | tf_op jit(solution)/shard_map/dot_general | solution.py:91
  141.6 77.4 %all-reduce.2 = (f32[512]{0:T(512)}, f32[512]{0:T(512)}) all-reduce(f32[512]{0:T(512)S(1)} %broadcast_multiply_fusion.1, f32[512]{0:T(512)S(1)} %broadcast_multiply_fusion), channel_id=1, replica_groups=mesh['dp'=2,'tm'=32,'space'=4] {'dp','tm','space'}, use_global_device_ids=true, to_apply=%region_6.7 | all-reduce | flops 1024 | bytes 8192 | tf_op jit(solution)/shard_map/psum | solution.py:115
  219.0 165.6 %reduce-scatter.5.cloned.1.call-done = f32[432,256]{1,0:T(8,128)} async-done(((f32[13824,256]{1,0:T(8,128)}), f32[432,256]{1,0:T(8,128)}) %reduce-scatter.5.cloned.1.call-update) | async-done | bytes 442384 | tf_op jit(solution)/shard_map/reduce_scatter | solution.py:116
  384.6 10.5 %fusion = f32[2,2,2,80,256]{4,3,2,1,0:T(8,128)S(1)} fusion(bf16[2,2,2,80,13824]{4,3,2,1,0:T(8,128)(2,1)} %copy-done.3, bf16[13824,256]{1,0:T(8,128)(2,1)} %param.7), kind=kOutput, calls=%fused_computation.1 | convolution fusion | flops 4529848320 | bytes 25427968 | tf_op jit(solution)/shard_map/dot_general | solution.py:86
  395.2 4.3 all_to_all.37
  400.3 33.2 %all-reduce.5.cloned.1.call-done = f32[432,256]{1,0:T(8,128)} async-done(((f32[432,256]{1,0:T(8,128)}), f32[432,256]{1,0:T(8,128)}) %all-reduce.5.cloned.1.call-update) | async-done | bytes 442384 | tf_op jit(solution)/shard_map/psum | solution.py:117
  433.5 1.8 copy.82
  (87 shorter events, 6.8 us)
Async XLA Ops:
  7.2 62.9 %reduce-scatter.3.cloned.1.call-start = ((), (), s32[]{:S(2)}) async-start(), calls=%async_computation.5 | async-start | bytes 1966080 | tf_op jit(solution)/shard_map/reduce_scatter | solution.py:105
  13.0 11.6 %collective-permute-start.3 = (bf16[2,2,2,80,256]{4,3,2,1,0:T(8,128)(2,1)S(1)}, bf16[2,2,2,80,256]{4,3,2,1,0:T(8,128)(2,1)S(1)}, u32[]{:S(2)}, u32[]{:S(2)}) collective-permute-start(bf16[2,2,2,80,256]{4,3,2,1,0:T(8,128)(2,1)S(1)} %bitcast.31), channel_id=1, source_target_pairs={{4,0},{8,4},{12,8},{16,12},{20,16},{24,20},{28,24},{32,28},{36,32}... | collective-permute-start | bytes 983048 | tf_op jit(solution)/shard_map/ppermute | solution.py:10
  24.7 15.0 %collective-permute-start.4 = (bf16[2,4,1,80,256]{4,3,2,1,0:T(8,128)(2,1)S(1)}, bf16[2,4,1,80,256]{4,3,2,1,0:T(8,128)(2,1)S(1)}, u32[]{:S(2)}, u32[]{:S(2)}) collective-permute-start(bf16[2,4,1,80,256]{4,3,2,1,0:T(8,128)(2,1)S(1)} %get-tuple-element.11), channel_id=1, source_target_pairs={{0,1},{1,2},{2,3},{4,5},{5,6},{6,7},{8,9},{9,10},{10,11},{12,13},{... | collective-permute-start | bytes 983048 | tf_op jit(solution)/shard_map/ppermute | solution.py:18
  28.2 11.6 %collective-permute-start.5 = (bf16[2,4,1,80,256]{4,3,2,1,0:T(8,128)(2,1)S(1)}, bf16[2,4,1,80,256]{4,3,2,1,0:T(8,128)(2,1)S(1)}, u32[]{:S(2)}, u32[]{:S(2)}) collective-permute-start(bf16[2,4,1,80,256]{4,3,2,1,0:T(8,128)(2,1)S(1)} %get-tuple-element.12), channel_id=1, source_target_pairs={{1,0},{2,1},{3,2},{5,4},{6,5},{7,6},{9,8},{10,9},{11,10},{13,12},{... | collective-permute-start | bytes 983048 | tf_op jit(solution)/shard_map/ppermute | solution.py:21
  40.7 2.2 slice-start
  41.4 2.6 slice-start.1
  44.0 5.9 %copy-start.1 = (bf16[1,2,2,80,512]{4,3,2,1,0:T(8,128)(2,1)S(1)}, bf16[1,2,2,80,512]{4,3,2,1,0:T(8,128)(2,1)}, u32[]{:S(2)}) copy-start(bf16[1,2,2,80,512]{4,3,2,1,0:T(8,128)(2,1)} %param.5) | copy-start | bytes 983044
  44.0 26.1 %copy-start.4 = (f32[512]{0:T(512)S(1)}, f32[512]{0:T(512)}, u32[]{:S(2)}) copy-start(f32[512]{0:T(512)} %param.6) | copy-start | bytes 6148
  44.0 27.7 %copy-start.2 = (bf16[1,2,2,80,512]{4,3,2,1,0:T(8,128)(2,1)S(1)}, bf16[1,2,2,80,512]{4,3,2,1,0:T(8,128)(2,1)}, u32[]{:S(2)}) copy-start(bf16[1,2,2,80,512]{4,3,2,1,0:T(8,128)(2,1)} %param.9) | copy-start | bytes 983044
  49.8 69.8 %all-gather.2.cloned.1.call-start = ((), (), s32[]{:S(2)}) async-start(), calls=%async_computation.4 | async-start | bytes 3932160 | tf_op jit(solution)/shard_map/all_gather | solution.py:83
  74.1 11.6 %collective-permute-start = (bf16[1,2,2,80,512]{4,3,2,1,0:T(8,128)(2,1)S(1)}, bf16[1,2,2,80,512]{4,3,2,1,0:T(8,128)(2,1)S(1)}, u32[]{:S(2)}, u32[]{:S(2)}) collective-permute-start(bf16[1,2,2,80,512]{4,3,2,1,0:T(8,128)(2,1)S(1)} %get-tuple-element.16), channel_id=1, source_target_pairs={{0,4},{4,8},{8,12},{12,16},{16,20},{20,24},{24,28},{28,32},{32,36}... | collective-permute-start | bytes 983048 | tf_op jit(solution)/shard_map/ppermute | solution.py:10
  85.8 9.8 %collective-permute-start.1 = (bf16[1,4,1,80,512]{4,3,2,1,0:T(8,128)(2,1)S(1)}, bf16[1,4,1,80,512]{4,3,2,1,0:T(8,128)(2,1)S(1)}, u32[]{:S(2)}, u32[]{:S(2)}) collective-permute-start(bf16[1,4,1,80,512]{4,3,2,1,0:T(8,128)(2,1)S(1)} %get-tuple-element.13), channel_id=1, source_target_pairs={{0,1},{1,2},{2,3},{4,5},{5,6},{6,7},{8,9},{9,10},{10,11},{12,13},{... | collective-permute-start | bytes 983048 | tf_op jit(solution)/shard_map/ppermute | solution.py:18
  89.2 10.5 %collective-permute-start.2 = (bf16[1,4,1,80,512]{4,3,2,1,0:T(8,128)(2,1)S(1)}, bf16[1,4,1,80,512]{4,3,2,1,0:T(8,128)(2,1)S(1)}, u32[]{:S(2)}, u32[]{:S(2)}) collective-permute-start(bf16[1,4,1,80,512]{4,3,2,1,0:T(8,128)(2,1)S(1)} %get-tuple-element.14), channel_id=1, source_target_pairs={{1,0},{2,1},{3,2},{5,4},{6,5},{7,6},{9,8},{10,9},{11,10},{13,12},{... | collective-permute-start | bytes 983048 | tf_op jit(solution)/shard_map/ppermute | solution.py:21
  101.0 283.7 %reduce-scatter.5.cloned.1.call-start = ((), (), s32[]{:S(2)}) async-start(), calls=%async_computation.6 | async-start | bytes 14598144 | tf_op jit(solution)/shard_map/reduce_scatter | solution.py:116
  119.6 3.8 copy-start
  126.4 6.1 %copy-start.3 = (bf16[2,2,2,80,13824]{4,3,2,1,0:T(8,128)(2,1)}, bf16[2,2,2,80,13824]{4,3,2,1,0:T(8,128)(2,1)S(1)}, u32[]{:S(2)}) copy-start(bf16[2,2,2,80,13824]{4,3,2,1,0:T(8,128)(2,1)S(1)} %slice_dynamic-update-slice_fusion.9) | copy-start | bytes 53084164
  141.5 292.0 %all-reduce.5.cloned.1.call-start = ((), (), s32[]{:S(2)}) async-start(), calls=%async_computation.7 | async-start | bytes 884736 | tf_op jit(solution)/shard_map/psum | solution.py:117
  384.6 14.9 %copy-start.5 = (f32[512]{0:T(512)S(1)}, f32[512]{0:T(512)}, u32[]{:S(2)}) copy-start(f32[512]{0:T(512)} %param.8) | copy-start | bytes 6148
Sparse Core Ops, SparseCore 0:
  50.0 20.0 reduce-scatter.2
  101.1 18.5 all-gather.1
  141.6 242.9 reduce-scatter.4
  386.8 46.6 all-reduce.4
where the time goes:
time: 443 us; the launch traced here: 442 us
  waiting for transfers between devices  262 us (59%)
  blocking collectives  85.8 us (19%)
  local copies, waits for them, and re-layouts  29.6 us (7%)
  matrix products  25.3 us (6%)
  starting transfers between devices  17.2 us (4%)
  between operations  14.4 us (3%)
  other arithmetic  7.21 us (2%)
    reduce_scatter x1, waiting for transfers between devices, on_device(): lax.psum_scatter(kernel_local, 'tm', scatter_dimension=0, tiled=True)  166 us
    psum x1, blocking collectives, on_device(): lax.psum((gain_local, bias_local), ('dp', 'tm', 'space'))  77.4 us
    psum x1, waiting for transfers between devices, on_device(): kernel_grad = lax.psum(row_part, 'space')  33.2 us
    reduce_scatter x1, waiting for transfers between devices, on_device(): lax.psum_scatter(partial_grad, 'dp', scatter_dimension=0, tiled=True)  20 us
    unnamed x69, local copies, waits for them, and re-layouts  18.6 us
    all_gather x1, waiting for transfers between devices, on_device(): act_pair = lax.all_gather(act_ext, 'dp', axis=0, tiled=True)  18.5 us
    ppermute x2, waiting for transfers between devices, shifted(): return lax.ppermute(block, axis, route)  15.8 us
    dot_general x1, matrix products, on_device(): conv_part = jnp.dot(act_taps, kernel, preferred_element_type=jnp.float32)  10.5 us
  transfers between devices with their start and end apart: 10, of which 8 were waited for; matrix products, arithmetic and copies ran while one was open for 5% of the time, Pallas kernels for 0%

commit v1 on v0

--- a/solution.py
+++ b/solution.py
@@ -114,7 +114,11 @@
     )
     gain_grad, bias_grad = lax.psum((gain_local, bias_local), ("dp", "tm", "space"))
     row_part = lax.psum_scatter(kernel_local, "tm", scatter_dimension=0, tiled=True)
-    kernel_grad = lax.psum(row_part, "space")
+    kernel_grad = row_part
+    for hop in (1, 2):
+        kernel_grad = kernel_grad + lax.ppermute(
+            kernel_grad, "space", [(dev, dev ^ hop) for dev in range(4)]
+        )
     return (block_out, latent_grad.astype(jnp.bfloat16), kernel_grad, gain_grad, bias_grad)
 
 

time: 443 us -> 489 us (1.10)
  waiting for transfers between devices: 262 us -> 307 us
    reduce_scatter x1, waiting for transfers between devices: 166 us -> 243 us  [on_device(): lax.psum_scatter(kernel_local, 'tm', scatter_dimension=0, tiled=True)]
    psum x1 -> x0, waiting for transfers between devices: 33.2 us -> none  [on_device(): kernel_grad = lax.psum(row_part, 'space')]
    unnamed x69 -> x68, local copies, waits for them, and re-layouts: 18.6 us -> 16.8 us
  transfers between devices with their start and end apart: 10 -> 11, of which waited for: 8 -> 7; matrix products, arithmetic and copies ran while one was open for 5% -> 5% of each run, Pallas kernels for 0% -> 0%
where the time goes in v1:
time: 489 us; the launch traced here: 486 us
  waiting for transfers between devices  307 us (63%)
  blocking collectives  82.2 us (17%)
  local copies, waits for them, and re-layouts  27.8 us (6%)
  matrix products  25.3 us (5%)
  starting transfers between devices  20.8 us (4%)
  between operations  14.3 us (3%)
  other arithmetic  9.1 us (2%)
    reduce_scatter x1, waiting for transfers between devices, on_device(): lax.psum_scatter(kernel_local, 'tm', scatter_dimension=0, tiled=True)  243 us
    psum x1, blocking collectives, on_device(): lax.psum((gain_local, bias_local), ('dp', 'tm', 'space'))  73.8 us
    reduce_scatter x1, waiting for transfers between devices, on_device(): lax.psum_scatter(partial_grad, 'dp', scatter_dimension=0, tiled=True)  20 us
    all_gather x1, waiting for transfers between devices, on_device(): act_pair = lax.all_gather(act_ext, 'dp', axis=0, tiled=True)  18.5 us
    unnamed x68, local copies, waits for them, and re-layouts  16.8 us
    ppermute x2, waiting for transfers between devices, shifted(): return lax.ppermute(block, axis, route)  15.8 us
    dot_general x1, matrix products, on_device(): conv_part = jnp.dot(act_taps, kernel, preferred_element_type=jnp.float32)  10.5 us
    transpose x1, local copies, waits for them, and re-layouts, on_device(): jnp.transpose(kernel.reshape(-1, chans, half_cols), (0, 2, 1))  10.3 us
  transfers between devices with their start and end apart: 11, of which 7 were waited for; matrix products, arithmetic and copies ran while one was open for 5% of the time, Pallas kernels for 0%

profile of v1, /device:TPU:8, one launch (start us, length us, event | category | flops | bytes accessed | tf_op | source)
XLA Modules:
  0.0 486.0 jit_solution(14266272378136626255)
XLA Ops:
  7.2 1.3 copy.20
  8.5 4.2 all_to_all.36
  13.0 4.1 collective-permute-start.3
  17.1 7.6 %collective-permute-done.3 = bf16[2,2,2,80,256]{4,3,2,1,0:T(8,128)(2,1)S(1)} collective-permute-done((bf16[2,2,2,80,256]{4,3,2,1,0:T(8,128)(2,1)S(1)}, bf16[2,2,2,80,256]{4,3,2,1,0:T(8,128)(2,1)S(1)}, u32[]{:S(2)}, u32[]{:S(2)}) %collective-permute-start.3) | collective-permute-done | bytes 327712 | tf_op jit(solution)/shard_map/ppermute | solution.py:10
  24.7 3.4 collective-permute-start.4
  28.2 1.3 collective-permute-start.5
  29.5 10.3 %copy.23 = bf16[27,256,512]{2,1,0:T(8,128)(2,1)} copy(bf16[27,256,512]{1,2,0:T(8,128)(2,1)} %bitcast.37) | data formatting | bytes 14155776 | tf_op jit(solution)/shard_map/transpose | solution.py:99
  42.9 1.1 slice-done.1
  44.0 5.8 %fusion.31 = f32[2,2,2,80,512]{4,3,2,1,0:T(8,128)} fusion(bf16[2,2,2,80,6912]{4,3,2,1,0:T(8,128)(2,1)S(1)} %slice_dynamic-update-slice_fusion.27, bf16[6912,512,1,1,1]{1,0,4,3,2:T(8,128)(2,1)S(1)} %bitcast.40), kind=kOutput, calls=%fused_computation.109 | convolution fusion | flops 4529848320 | bytes 17235968 | tf_op jit(solution)/shard_map/dot_general | solution.py:103
  50.1 20.0 %reduce-scatter.3.cloned.1.call-done = f32[1,2,2,80,512]{4,3,2,1,0:T(8,128)} async-done(((f32[2,2,2,80,512]{4,3,2,1,0:T(8,128)}), f32[1,2,2,80,512]{4,3,2,1,0:T(8,128)}) %reduce-scatter.3.cloned.1.call-update) | async-done | bytes 655376 | tf_op jit(solution)/shard_map/reduce_scatter | solution.py:105
  70.1 1.6 fusion.23
  71.7 2.4 fusion.13
  74.1 3.4 collective-permute-start
  77.5 8.2 %collective-permute-done = bf16[1,2,2,80,512]{4,3,2,1,0:T(8,128)(2,1)S(1)} collective-permute-done((bf16[1,2,2,80,512]{4,3,2,1,0:T(8,128)(2,1)S(1)}, bf16[1,2,2,80,512]{4,3,2,1,0:T(8,128)(2,1)S(1)}, u32[]{:S(2)}, u32[]{:S(2)}) %collective-permute-start) | collective-permute-done | bytes 327712 | tf_op jit(solution)/shard_map/ppermute | solution.py:10
  85.8 3.4 collective-permute-start.1
  89.2 1.3 collective-permute-start.2
  90.5 5.1 %collective-permute-done.1 = bf16[1,4,1,80,512]{4,3,2,1,0:T(8,128)(2,1)S(1)} collective-permute-done((bf16[1,4,1,80,512]{4,3,2,1,0:T(8,128)(2,1)S(1)}, bf16[1,4,1,80,512]{4,3,2,1,0:T(8,128)(2,1)S(1)}, u32[]{:S(2)}, u32[]{:S(2)}) %collective-permute-start.1) | collective-permute-done | bytes 327712 | tf_op jit(solution)/shard_map/ppermute | solution.py:18
  95.6 4.1 collective-permute-done.2
  99.7 1.2 pad_maximum_fusion
  101.2 18.5 %all-gather.2.cloned.1.call-done = bf16[2,4,4,80,512]{4,3,2,1,0:T(8,128)(2,1)} async-done(((bf16[1,4,4,80,512]{4,3,2,1,0:T(8,128)(2,1)}), bf16[2,4,4,80,512]{4,3,2,1,0:T(8,128)(2,1)}) %all-gather.2.cloned.1.call-update) | async-done | bytes 2621456 | tf_op jit(solution)/shard_map/all_gather | solution.py:83
  119.6 1.4 slice_dynamic-update-slice_fusion.26
  121.0 1.1 slice_dynamic-update-slice_fusion.8
  122.2 1.2 slice_dynamic-update-slice_fusion.25
  126.4 6.1 %copy-done.3 = bf16[2,2,2,80,13824]{4,3,2,1,0:T(8,128)(2,1)} copy-done((bf16[2,2,2,80,13824]{4,3,2,1,0:T(8,128)(2,1)}, bf16[2,2,2,80,13824]{4,3,2,1,0:T(8,128)(2,1)S(1)}, u32[]{:S(2)}) %copy-start.3) | copy-done | bytes 17694744
  132.5 9.0 %convolution_multiply_fusion = f32[13824,256]{1,0:T(8,128)} fusion(bf16[640,13824]{1,0:T(8,128)(2,1)S(1)} %bitcast.44, bf16[640,256]{1,0:T(8,128)(2,1)S(1)} %bitcast.36), kind=kOutput, calls=%fused_computation | convolution fusion | flops 4533387264 | bytes 32178176 | tf_op jit(solution)/shard_map/dot_general | solution.py:91
  141.5 243.0 %reduce-scatter.5.cloned.1.call-done = f32[432,256]{1,0:T(8,128)} async-done(((f32[13824,256]{1,0:T(8,128)}), f32[432,256]{1,0:T(8,128)}) %reduce-scatter.5.cloned.1.call-update) | async-done | bytes 442384 | tf_op jit(solution)/shard_map/reduce_scatter | solution.py:116
  384.4 1.8 collective-permute-start.6
  386.2 73.8 %all-reduce.2 = (f32[512]{0:T(512)}, f32[512]{0:T(512)}) all-reduce(f32[512]{0:T(512)S(1)} %broadcast_multiply_fusion.1, f32[512]{0:T(512)S(1)} %broadcast_multiply_fusion), channel_id=1, replica_groups=mesh['dp'=2,'tm'=32,'space'=4] {'dp','tm','space'}, use_global_device_ids=true, to_apply=%region_5.6 | all-reduce | flops 1024 | bytes 8192 | tf_op jit(solution)/shard_map/psum | solution.py:115
  460.0 1.1 add.59
  461.0 1.9 collective-permute-start.7
  462.9 10.5 %fusion = f32[2,2,2,80,256]{4,3,2,1,0:T(8,128)S(1)} fusion(bf16[2,2,2,80,13824]{4,3,2,1,0:T(8,128)(2,1)} %copy-done.3, bf16[13824,256]{1,0:T(8,128)(2,1)} %param.7), kind=kOutput, calls=%fused_computation.1 | convolution fusion | flops 4529848320 | bytes 25427968 | tf_op jit(solution)/shard_map/dot_general | solution.py:86
  473.4 4.3 all_to_all.37
  (89 shorter events, 8.5 us)
Async XLA Ops:
  7.2 62.9 %reduce-scatter.3.cloned.1.call-start = ((), (), s32[]{:S(2)}) async-start(), calls=%async_computation.5 | async-start | bytes 1966080 | tf_op jit(solution)/shard_map/reduce_scatter | solution.py:105
  13.0 11.6 %collective-permute-start.3 = (bf16[2,2,2,80,256]{4,3,2,1,0:T(8,128)(2,1)S(1)}, bf16[2,2,2,80,256]{4,3,2,1,0:T(8,128)(2,1)S(1)}, u32[]{:S(2)}, u32[]{:S(2)}) collective-permute-start(bf16[2,2,2,80,256]{4,3,2,1,0:T(8,128)(2,1)S(1)} %bitcast.31), channel_id=1, source_target_pairs={{4,0},{8,4},{12,8},{16,12},{20,16},{24,20},{28,24},{32,28},{36,32}... | collective-permute-start | bytes 983048 | tf_op jit(solution)/shard_map/ppermute | solution.py:10
  24.7 15.0 %collective-permute-start.4 = (bf16[2,4,1,80,256]{4,3,2,1,0:T(8,128)(2,1)S(1)}, bf16[2,4,1,80,256]{4,3,2,1,0:T(8,128)(2,1)S(1)}, u32[]{:S(2)}, u32[]{:S(2)}) collective-permute-start(bf16[2,4,1,80,256]{4,3,2,1,0:T(8,128)(2,1)S(1)} %get-tuple-element.11), channel_id=1, source_target_pairs={{0,1},{1,2},{2,3},{4,5},{5,6},{6,7},{8,9},{9,10},{10,11},{12,13},{... | collective-permute-start | bytes 983048 | tf_op jit(solution)/shard_map/ppermute | solution.py:18
  28.2 11.6 %collective-permute-start.5 = (bf16[2,4,1,80,256]{4,3,2,1,0:T(8,128)(2,1)S(1)}, bf16[2,4,1,80,256]{4,3,2,1,0:T(8,128)(2,1)S(1)}, u32[]{:S(2)}, u32[]{:S(2)}) collective-permute-start(bf16[2,4,1,80,256]{4,3,2,1,0:T(8,128)(2,1)S(1)} %get-tuple-element.12), channel_id=1, source_target_pairs={{1,0},{2,1},{3,2},{5,4},{6,5},{7,6},{9,8},{10,9},{11,10},{13,12},{... | collective-permute-start | bytes 983048 | tf_op jit(solution)/shard_map/ppermute | solution.py:21
  40.7 2.2 slice-start
  41.4 2.6 slice-start.1
  44.0 5.9 %copy-start.1 = (bf16[1,2,2,80,512]{4,3,2,1,0:T(8,128)(2,1)S(1)}, bf16[1,2,2,80,512]{4,3,2,1,0:T(8,128)(2,1)}, u32[]{:S(2)}) copy-start(bf16[1,2,2,80,512]{4,3,2,1,0:T(8,128)(2,1)} %param.5) | copy-start | bytes 983044
  44.0 26.1 %copy-start.4 = (f32[512]{0:T(512)S(1)}, f32[512]{0:T(512)}, u32[]{:S(2)}) copy-start(f32[512]{0:T(512)} %param.6) | copy-start | bytes 6148
  44.0 27.7 %copy-start.2 = (bf16[1,2,2,80,512]{4,3,2,1,0:T(8,128)(2,1)S(1)}, bf16[1,2,2,80,512]{4,3,2,1,0:T(8,128)(2,1)}, u32[]{:S(2)}) copy-start(bf16[1,2,2,80,512]{4,3,2,1,0:T(8,128)(2,1)} %param.9) | copy-start | bytes 983044
  49.8 69.8 %all-gather.2.cloned.1.call-start = ((), (), s32[]{:S(2)}) async-start(), calls=%async_computation.4 | async-start | bytes 3932160 | tf_op jit(solution)/shard_map/all_gather | solution.py:83
  74.1 11.6 %collective-permute-start = (bf16[1,2,2,80,512]{4,3,2,1,0:T(8,128)(2,1)S(1)}, bf16[1,2,2,80,512]{4,3,2,1,0:T(8,128)(2,1)S(1)}, u32[]{:S(2)}, u32[]{:S(2)}) collective-permute-start(bf16[1,2,2,80,512]{4,3,2,1,0:T(8,128)(2,1)S(1)} %get-tuple-element.16), channel_id=1, source_target_pairs={{0,4},{4,8},{8,12},{12,16},{16,20},{20,24},{24,28},{28,32},{32,36}... | collective-permute-start | bytes 983048 | tf_op jit(solution)/shard_map/ppermute | solution.py:10
  85.8 9.8 %collective-permute-start.1 = (bf16[1,4,1,80,512]{4,3,2,1,0:T(8,128)(2,1)S(1)}, bf16[1,4,1,80,512]{4,3,2,1,0:T(8,128)(2,1)S(1)}, u32[]{:S(2)}, u32[]{:S(2)}) collective-permute-start(bf16[1,4,1,80,512]{4,3,2,1,0:T(8,128)(2,1)S(1)} %get-tuple-element.13), channel_id=1, source_target_pairs={{0,1},{1,2},{2,3},{4,5},{5,6},{6,7},{8,9},{9,10},{10,11},{12,13},{... | collective-permute-start | bytes 983048 | tf_op jit(solution)/shard_map/ppermute | solution.py:18
  89.2 10.5 %collective-permute-start.2 = (bf16[1,4,1,80,512]{4,3,2,1,0:T(8,128)(2,1)S(1)}, bf16[1,4,1,80,512]{4,3,2,1,0:T(8,128)(2,1)S(1)}, u32[]{:S(2)}, u32[]{:S(2)}) collective-permute-start(bf16[1,4,1,80,512]{4,3,2,1,0:T(8,128)(2,1)S(1)} %get-tuple-element.14), channel_id=1, source_target_pairs={{1,0},{2,1},{3,2},{5,4},{6,5},{7,6},{9,8},{10,9},{11,10},{13,12},{... | collective-permute-start | bytes 983048 | tf_op jit(solution)/shard_map/ppermute | solution.py:21
  100.9 283.5 %reduce-scatter.5.cloned.1.call-start = ((), (), s32[]{:S(2)}) async-start(), calls=%async_computation.6 | async-start | bytes 14598144 | tf_op jit(solution)/shard_map/reduce_scatter | solution.py:116
  119.6 3.8 copy-start
  126.4 6.1 %copy-start.3 = (bf16[2,2,2,80,13824]{4,3,2,1,0:T(8,128)(2,1)}, bf16[2,2,2,80,13824]{4,3,2,1,0:T(8,128)(2,1)S(1)}, u32[]{:S(2)}) copy-start(bf16[2,2,2,80,13824]{4,3,2,1,0:T(8,128)(2,1)S(1)} %slice_dynamic-update-slice_fusion.9) | copy-start | bytes 53084164
  384.4 75.5 %collective-permute-start.6 = (f32[432,256]{1,0:T(8,128)}, f32[432,256]{1,0:T(8,128)S(1)}, u32[]{:S(2)}, u32[]{:S(2)}) collective-permute-start(f32[432,256]{1,0:T(8,128)} %reduce-scatter.5.cloned.1.call-done), channel_id=1, source_target_pairs={{0,1},{1,0},{2,3},{3,2},{4,5},{5,4},{6,7},{7,6},{8,9},{9,8},{10,11... | collective-permute-start | bytes 1327112 | tf_op jit(solution)/shard_map/ppermute | solution.py:119
  461.0 16.7 %copy-start.5 = (f32[512]{0:T(512)S(1)}, f32[512]{0:T(512)}, u32[]{:S(2)}) copy-start(f32[512]{0:T(512)} %param.8) | copy-start | bytes 6148
  461.0 17.6 %collective-permute-start.7 = (f32[432,256]{1,0:T(8,128)S(1)}, f32[432,256]{1,0:T(8,128)S(1)}, u32[]{:S(2)}, u32[]{:S(2)}) collective-permute-start(f32[432,256]{1,0:T(8,128)S(1)} %add.59), channel_id=1, source_target_pairs={{0,2},{1,3},{2,0},{3,1},{4,6},{5,7},{6,4},{7,5},{8,10},{9,11},{10,... | collective-permute-start | bytes 1327112 | tf_op jit(solution)/shard_map/ppermute | solution.py:119
Sparse Core Ops, SparseCore 0:
  49.9 20.0 reduce-scatter.2
  101.1 18.5 all-gather.1
  141.6 242.8 reduce-scatter.4
